TPU v7x, 32 devices: a whole 2x2x4 slice. The times are simulated.
32 devices in a mesh: dp: 4 (over y, core), bucket: 8 (over z, x).
Axes of the slice: x: 2, y: 2, z: 4, core: 2. Of those that a mesh axis runs over, the one named last changes fastest.
Arguments:
- frames: bfloat16 [49152, 512], P(('dp', 'bucket')), may hold values from -60 to 60, as said below
- lengths: int32 [4, 256], P('dp'), may hold values from 1 to 48, as said below
- owners: int32 [4, 256], P('dp'), may hold values from 0 to 7, as said below
- upstream: bfloat16 [24576, 512], P(('dp', 'bucket')), may hold values from -6 to 6
- ln_gain: float32 [512], replicated, may hold values from 0.1 to 1.9
- w_in: bfloat16 [512, 1024], replicated, may hold values from -0.25 to 0.25
- w_dw: float32 [512, 31], replicated, may hold values from -1 to 1
- bn_gain: float32 [512], replicated, may hold values from 0.1 to 1.9
- bn_bias: float32 [512], replicated, may hold values from -3 to 3
- w_out: bfloat16 [512, 512], replicated, may hold values from -0.25 to 0.25
Outputs:
- out_frames: bfloat16 [24576, 512], P(('dp', 'bucket'))
- grad_frames: bfloat16 [49152, 512], P(('dp', 'bucket'))
- grad_w_in: float32 [512, 1024], P('bucket')
- grad_w_out: float32 [512, 512], P('bucket')
- grad_w_dw: float32 [512, 31], P('bucket')
- grad_ln_gain: float32 [512], P('bucket')
- grad_bn_gain: float32 [512], replicated
- grad_bn_bias: float32 [512], replicated
Inputs may be any that keep to these rules, and one draw needn't show every extreme that they name: `frames`: frame rows past an utterance's length are not read. In each group every owner receives exactly 4 utterances from each loader shard, their lengths sum to exactly 768 with one of exactly 48, and the lengths an owner receives do not fall with the loader index. `owners`: in each group and loader shard every owner index appears exactly 4 times.
All inputs are finite; a program needn't handle non-finite values.
Results may differ from a plain program's by a relative error of at most 0.013.
Values may be sent and summed in bfloat16 or wider, within the bound.
A program may use at most 128 MiB of HBM per device.

v0:
```python
import jax
import jax.numpy as jnp
from jax import lax
from jax.sharding import PartitionSpec as P

EPSILON = 1e-05


def normalize_rows(frame_rows, ln_gain):
    values = frame_rows.astype(jnp.float32)
    centred = values - jnp.mean(values, axis=1, keepdims=True)
    inverse = lax.rsqrt(jnp.mean(centred * centred, axis=1, keepdims=True) + EPSILON)
    normed = centred * inverse
    return ((normed * ln_gain).astype(jnp.bfloat16), normed, inverse)


def normalize_back(grad_h, normed, inverse, ln_gain):
    scaled = grad_h * ln_gain
    inner_sum = jnp.mean(scaled * normed, axis=1, keepdims=True)
    return inverse * (scaled - jnp.mean(scaled, axis=1, keepdims=True) - normed * inner_sum)


def conv_forward(gated_rows, segment, w_dw):
    width_half = w_dw.shape[1] // 2
    length_all = gated_rows.shape[1]
    padded = jnp.pad(gated_rows, ((0, 0), (width_half, width_half), (0, 0)))
    seg_pad = jnp.pad(segment, ((0, 0), (width_half, width_half)), constant_values=-1)
    result = jnp.zeros(gated_rows.shape, jnp.float32)
    for offset in range(w_dw.shape[1]):
        same_seg = (seg_pad[:, offset : offset + length_all] == segment)[:, :, None]
        shifted = padded[:, offset : offset + length_all].astype(jnp.float32)
        result = result + jnp.where(same_seg, shifted, 0.0) * w_dw[:, offset]
    return result


def conv_backward(grad_conv, gated_rows, segment, w_dw):
    width_half = w_dw.shape[1] // 2
    length_all = gated_rows.shape[1]
    padded = jnp.pad(gated_rows, ((0, 0), (width_half, width_half), (0, 0)))
    grad_pad = jnp.pad(grad_conv, ((0, 0), (width_half, width_half), (0, 0)))
    seg_pad = jnp.pad(segment, ((0, 0), (width_half, width_half)), constant_values=-1)
    grad_gated = jnp.zeros(grad_conv.shape, jnp.float32)
    grad_cols = []
    for offset in range(w_dw.shape[1]):
        same_fwd = (seg_pad[:, offset : offset + length_all] == segment)[:, :, None]
        shifted = jnp.where(
            same_fwd, padded[:, offset : offset + length_all].astype(jnp.float32), 0.0
        )
        grad_cols.append(jnp.sum(shifted * grad_conv, axis=(0, 1)))
        back_start = 2 * width_half - offset
        same_back = (seg_pad[:, back_start : back_start + length_all] == segment)[:, :, None]
        grad_gated = (
            grad_gated
            + jnp.where(same_back, grad_pad[:, back_start : back_start + length_all], 0.0)
            * w_dw[:, offset]
        )
    return (grad_gated, jnp.stack(grad_cols, axis=1))


def local(frames, lengths, owners, upstream, ln_gain, w_in, w_dw, bn_gain, bn_bias, w_out):
    loaders = lax.axis_size("bucket")
    own_index = lax.axis_index("bucket")
    feature_count = frames.shape[1]
    slot_count = lengths.shape[1] // loaders
    span_max = frames.shape[0] // slot_count
    pair_count = slot_count // loaders
    own_rows = upstream.shape[0]
    total_frames = float(own_rows * loaders * lax.axis_size("dp"))
    lens_all = lengths[0].reshape(loaders, slot_count)
    dest_all = owners[0].reshape(loaders, slot_count)
    owner_ids = jnp.arange(loaders, dtype=jnp.int32)
    onehot = (dest_all[:, :, None] == owner_ids[None, None, :]).astype(jnp.int32)
    earlier = jnp.cumsum(onehot, axis=1) - onehot
    ranking = jnp.sum(earlier * onehot, axis=2)
    send_pos = dest_all * pair_count + ranking
    my_pos = lax.dynamic_index_in_dim(send_pos, own_index, 0, keepdims=False)
    send_order = (
        jnp.zeros((slot_count,), jnp.int32).at[my_pos].set(jnp.arange(slot_count, dtype=jnp.int32))
    )
    slot_frames = frames.reshape(slot_count, span_max, feature_count)
    outgoing = jnp.take(slot_frames, send_order, axis=0).reshape(
        loaders, pair_count, span_max, feature_count
    )
    incoming = lax.all_to_all(outgoing, "bucket", split_axis=0, concat_axis=0, tiled=True)
    incoming_rows = incoming.reshape(slot_count * span_max, feature_count)
    pair_ids = jnp.arange(pair_count, dtype=jnp.int32)
    to_me = (dest_all == own_index)[:, :, None] & (ranking[:, :, None] == pair_ids[None, None, :])
    recv_lens = jnp.sum(jnp.where(to_me, lens_all[:, :, None], 0), axis=1).reshape(-1)
    starts = jnp.cumsum(recv_lens) - recv_lens
    position = jnp.arange(span_max, dtype=jnp.int32)
    slot_valid = position[None, :] < recv_lens[:, None]
    row_ids = jnp.arange(own_rows, dtype=jnp.int32)
    row_slot = jnp.sum((starts[None, :] <= row_ids[:, None]).astype(jnp.int32), axis=1) - 1
    row_offset = row_ids - jnp.take(starts, row_slot)
    packed_source = row_slot * span_max + row_offset
    slot_target = jnp.minimum(
        jnp.where(slot_valid, starts[:, None] + position[None, :], own_rows - 1), own_rows - 1
    ).reshape(-1)
    slot_valid_flat = slot_valid.reshape(-1)
    segment = jnp.broadcast_to(
        jnp.arange(slot_count, dtype=jnp.int32)[:, None], (slot_count, span_max)
    )
    work_grad = jnp.where(slot_valid_flat[:, None], jnp.take(upstream, slot_target, axis=0), 0)
    group_count = segment.shape[0]
    group_length = segment.shape[1]
    normed_h, normed, inverse = normalize_rows(incoming_rows, ln_gain)
    projected = jnp.dot(normed_h, w_in, preferred_element_type=jnp.float32)
    linear = projected[:, :feature_count]
    gate_sig = jax.nn.sigmoid(projected[:, feature_count:])
    gated_rows = jnp.where(slot_valid_flat[:, None], linear * gate_sig, 0.0).astype(jnp.bfloat16)
    gated_blocks = gated_rows.reshape(group_count, group_length, feature_count)
    conv_rows = conv_forward(gated_blocks, segment, w_dw).reshape(-1, feature_count)
    masked = jnp.where(slot_valid_flat[:, None], conv_rows, 0.0)
    first_sum, second_sum = lax.psum(
        (jnp.sum(masked, axis=0), jnp.sum(masked * masked, axis=0)), ("dp", "bucket")
    )
    centre = first_sum / total_frames
    variance = second_sum / total_frames - centre * centre
    bn_inverse = lax.rsqrt(variance + EPSILON)
    bn_normed = (conv_rows - centre) * bn_inverse
    bn_value = bn_normed * bn_gain + bn_bias
    bn_sig = jax.nn.sigmoid(bn_value)
    swished = (bn_value * bn_sig).astype(jnp.bfloat16)
    out_rows = jnp.dot(swished, w_out, preferred_element_type=jnp.float32).astype(jnp.bfloat16)
    out_frames = jnp.take(out_rows, packed_source, axis=0)
    grad_wout = jnp.einsum("rd,re->de", swished, work_grad, preferred_element_type=jnp.float32)
    grad_swish = jnp.einsum("re,de->rd", work_grad, w_out, preferred_element_type=jnp.float32)
    grad_bn_rows = grad_swish * (bn_sig * (1.0 + bn_value * (1.0 - bn_sig)))
    bias_total, gain_total = lax.psum(
        (jnp.sum(grad_bn_rows, axis=0), jnp.sum(grad_bn_rows * bn_normed, axis=0)), ("dp", "bucket")
    )
    grad_conv = jnp.where(
        slot_valid_flat[:, None],
        bn_gain
        * bn_inverse
        * (grad_bn_rows - bias_total / total_frames - bn_normed * (gain_total / total_frames)),
        0.0,
    )
    grad_gated, grad_wdw = conv_backward(
        grad_conv.reshape(group_count, group_length, feature_count), gated_blocks, segment, w_dw
    )
    grad_gated = jnp.where(slot_valid_flat[:, None], grad_gated.reshape(-1, feature_count), 0.0)
    grad_proj = jnp.concatenate(
        [grad_gated * gate_sig, grad_gated * linear * gate_sig * (1.0 - gate_sig)], axis=1
    ).astype(jnp.bfloat16)
    grad_win = jnp.einsum("rd,rf->df", normed_h, grad_proj, preferred_element_type=jnp.float32)
    grad_h = jnp.einsum("rf,df->rd", grad_proj, w_in, preferred_element_type=jnp.float32)
    grad_ln = jnp.sum(grad_h * normed, axis=0)
    grad_work = jnp.where(
        slot_valid_flat[:, None], normalize_back(grad_h, normed, inverse, ln_gain), 0.0
    ).astype(jnp.bfloat16)
    returned = lax.all_to_all(
        grad_work.reshape(loaders, pair_count, span_max, feature_count),
        "bucket",
        split_axis=0,
        concat_axis=0,
        tiled=True,
    )
    grad_frames = jnp.take(
        returned.reshape(slot_count, span_max, feature_count), my_pos, axis=0
    ).reshape(-1, feature_count)
    row_sums = (
        lax.psum_scatter(grad_win, "bucket", scatter_dimension=0, tiled=True),
        lax.psum_scatter(grad_wout, "bucket", scatter_dimension=0, tiled=True),
        lax.psum_scatter(grad_wdw, "bucket", scatter_dimension=0, tiled=True),
        lax.psum_scatter(grad_ln, "bucket", scatter_dimension=0, tiled=True),
    )
    shares = (
        lax.psum(row_sums[0].astype(jnp.bfloat16), "dp").astype(jnp.float32),
        lax.psum(row_sums[1].astype(jnp.bfloat16), "dp").astype(jnp.float32),
        lax.psum(row_sums[2].astype(jnp.bfloat16), "dp").astype(jnp.float32),
        lax.psum(row_sums[3].astype(jnp.bfloat16), "dp").astype(jnp.float32),
    )
    return (
        out_frames,
        grad_frames,
        shares[0],
        shares[1],
        shares[2],
        shares[3],
        gain_total,
        bias_total,
    )


def solution(mesh):
    placed = (
        P(("dp", "bucket"), None),
        P("dp", None),
        P("dp", None),
        P(("dp", "bucket"), None),
        P(),
        P(),
        P(),
        P(),
        P(),
        P(),
    )
    return jax.shard_map(
        local,
        mesh=mesh,
        in_specs=placed,
        out_specs=(
            P(("dp", "bucket"), None),
            P(("dp", "bucket"), None),
            P("bucket", None),
            P("bucket", None),
            P("bucket", None),
            P("bucket"),
            P(),
            P(),
        ),
        check_vma=False,
    )
```

profile of v0, /device:TPU:0, one launch (start us, length us, event | category | flops | bytes accessed | tf_op | source)
XLA Modules:
  0.0 468.8 jit_solution(478238532868027686)
XLA Ops:
  7.2 0.5 broadcast.618
  7.7 1.3 reduce.68
  9.2 0.7 fusion.118
  10.0 0.7 scatter_custom_fusion
  10.8 1.8 gather_fusion.2
  12.6 2.8 broadcast_select_fusion.1
  15.4 7.3 %all-to-all-start = ((bf16[8,4,48,512]{3,2,1,0:T(8,128)(2,1)}), bf16[8,4,48,512]{3,2,1,0:T(8,128)(2,1)}, u32[]{:S(2)}, u32[]{:S(2)}) async-start(bf16[8,4,48,512]{3,2,1,0:T(8,128)(2,1)} %bitcast.243), calls=%async_computation | async-start | bytes 3145728 | tf_op jit(solution)/shard_map/all_to_all | solution.py:84
  22.7 0.7 reduce.69
  23.5 0.1 select_reduce_fusion.1
  23.9 0.1 lt.126
  24.1 0.1 reduce.7
  24.5 5.4 %gather_fusion.1 = bf16[1536,512]{1,0:T(8,128)(2,1)} fusion(bf16[768,512]{1,0:T(8,128)(2,1)S(1)} %copy-done.1, s32[2048]{0:T(1024)S(1)} %pad_clamp_fusion), kind=kCustom, calls=%fused_computation.3 | custom fusion | bytes 3151872 | tf_op jit(solution)/shard_map/jit(_take)/gather | solution.py:103
  30.1 29.7 %all-to-all-done = bf16[8,4,48,512]{3,2,1,0:T(8,128)(2,1)} async-done(((bf16[8,4,48,512]{3,2,1,0:T(8,128)(2,1)}), bf16[8,4,48,512]{3,2,1,0:T(8,128)(2,1)}, u32[]{:S(2)}, u32[]{:S(2)}) %all-to-all-start) | async-done | bytes 1572896 | tf_op jit(solution)/shard_map/all_to_all | solution.py:84
  59.8 1.7 convert_reduce_fusion
  61.6 2.1 multiply_reduce_fusion.35
  63.8 2.0 multiply_convert_fusion.3
  65.8 1.8 fusion.119
  68.0 1.4 select_convert_fusion.1
  69.4 0.9 copy-done.3
  70.6 20.7 %select_reduce_fusion = (f32[512]{0:T(512)S(1)}, f32[512]{0:T(512)S(1)}, f32[32,48,512]{2,1,0:T(8,128)}) fusion(pred[32,48]{1,0:T(8,128)(4,1)S(1)} %iota_compare_fusion.3, f32[512]{0:T(512)S(1)} %bitcast.355, pred[32,48]{1,0:T(8,128)(4,1)S(1)} %bitcast.323, f32[512]{0:T(512)S(1)} %bitcast.357, pred[32,48]{1,0:T(8,128)(4,1)S(1)} %bitcast.320, ...), kind=kLoop, calls=%fused_computation.243 | loop fusion | flops 99089408 | bytes 4833792 | tf_op jit(solution)/shard_map/reduce_sum | solution.py:115
  91.3 37.9 %all-reduce.4 = (f32[512]{0:T(512)S(1)}, f32[512]{0:T(512)S(1)}) all-reduce(f32[512]{0:T(512)S(1)} %get-tuple-element.42, f32[512]{0:T(512)S(1)} %get-tuple-element.41), channel_id=1, replica_groups=mesh['dp'=4,'bucket'=8] {'dp','bucket'}, use_global_device_ids=true, to_apply=%region_11.13 | all-reduce | flops 1024 | bytes 8192 | tf_op jit(solution)/shard_map/psum | solution.py:114
  129.2 4.2 multiply_convert_fusion.2
  133.4 4.3 fusion.111
  137.7 41.4 %all-reduce.3 = (f32[512]{0:T(512)S(1)}, f32[512]{0:T(512)S(1)}) all-reduce(f32[512]{0:T(512)S(1)} %get-tuple-element.45, f32[512]{0:T(512)S(1)} %get-tuple-element.44), channel_id=1, replica_groups=mesh['dp'=4,'bucket'=8] {'dp','bucket'}, use_global_device_ids=true, to_apply=%region_15.17 | all-reduce | flops 1024 | bytes 8192 | tf_op jit(solution)/shard_map/psum | solution.py:129
  179.0 0.6 copy-done.43
  179.6 5.5 %multiply_reduce_fusion.16 = (f32[512]{0:T(512)S(1)}, f32[1536,512]{1,0:T(8,128)S(1)}) fusion(f32[1536,512]{1,0:T(8,128)} %copy-done.4, f32[512]{0:T(512)S(1)} %get-tuple-element.164, f32[1536,512]{1,0:T(8,128)} %get-tuple-element.162, f32[512]{0:T(512)S(1)} %get-tuple-element.165, f32[512]{0:T(512)S(1)} %get-tuple-element.83, pred[1536]{0:T(1024)(128)(4,1)S(1)} %lt.126, ...), kind=kLoop, calls=%fused_computation.182 | loop fusion | flops 11009536 | bytes 15738368 | tf_op jit(solution)/shard_map/reduce_sum | solution.py:49
  185.2 1.9 multiply_reduce_fusion.29
  187.1 7.1 %multiply_reduce_fusion.10 = (f32[512]{0:T(512)S(1)}, f32[512]{0:T(512)S(1)}, f32[512]{0:T(512)S(1)}, f32[512]{0:T(512)S(1)}, f32[512]{0:T(512)S(1)}, /*index=5*...) fusion(f32[32,48,512]{2,1,0:T(8,128)S(1)} %bitcast.234, pred[32,48]{1,0:T(8,128)(4,1)S(1)} %bitcast.297, ...), kind=kLoop, calls=%fused_computation.176 | loop fusion | flops 28306944 | bytes 4750848 | tf_op jit(solution)/shard_map/reduce_sum | solution.py:49
  194.2 6.7 %multiply_reduce_fusion.20 = (f32[512]{0:T(512)S(1)}, f32[512]{0:T(512)S(1)}, f32[512]{0:T(512)S(1)}, f32[512]{0:T(512)S(1)}, f32[512]{0:T(512)S(1)}, /*index=5*...) fusion(f32[32,48,512]{2,1,0:T(8,128)S(1)} %bitcast.235, pred[32,48]{1,0:T(8,128)(4,1)S(1)} %bitcast.270, ...), kind=kLoop, calls=%fused_computation.186 | loop fusion | flops 28306944 | bytes 4750848 | tf_op jit(solution)/shard_map/reduce_sum | solution.py:49
  200.9 6.5 %multiply_reduce_fusion.1 = (f32[512]{0:T(512)S(1)}, f32[512]{0:T(512)S(1)}, f32[512]{0:T(512)S(1)}, f32[512]{0:T(512)S(1)}, f32[512]{0:T(512)S(1)}, /*index=5*/...) fusion(f32[32,48,512]{2,1,0:T(8,128)S(1)} %bitcast.236, pred[32,48]{1,0:T(8,128)(4,1)S(1)} %bitcast.324, ...), kind=kLoop, calls=%fused_computation.167 | loop fusion | flops 28306944 | bytes 4750848 | tf_op jit(solution)/shard_map/reduce_sum | solution.py:49
  207.4 0.1 stack.127
  207.5 0.8 copy.41
  208.5 4.0 fusion.110
  212.5 0.3 reduce-scatter.6.cloned.1.call-start
  212.8 49.1 %fusion.73 = f32[32,48,512]{2,1,0:T(8,128)} fusion(f32[32,48,512]{2,1,0:T(8,128)} %bitcast.237, f32[512]{0:T(512)S(1)} %bitcast.356, f32[512]{0:T(512)S(1)} %bitcast.358, f32[512]{0:T(512)S(1)} %bitcast.362, f32[512]{0:T(512)S(1)} %bitcast.364, f32[512]{0:T(512)S(1)} %bitcast.366, f32[512]{0:T(512)S(1)} %bitcast.368, f32[512]{0:T(512)S(1)} %bitcast.370, ...), kind=kLoop, calls=%fused_computation.139 | loop fusion | flops 71565312 | bytes 6401024 | tf_op jit(solution)/shard_map/add | solution.py:53
  261.9 4.7 %multiply_convert_fusion.1 = (bf16[1536,512]{1,0:T(8,128)(2,1)S(1)}, bf16[1536,512]{1,0:T(8,128)(2,1)S(1)}) fusion(f32[32,48,512]{2,1,0:T(8,128)} %fusion.73, pred[1536]{0:T(1024)(128)(4,1)S(1)} %lt.126, f32[1536,1024]{1,0:T(8,128)} %copy-done.3), kind=kLoop, calls=%fused_computation.201 | loop fusion | flops 8650752 | bytes 12584448 | tf_op jit(solution)/shard_map/convert.1
  266.6 1.1 copy-done.8
  267.7 3.2 fusion.95
  270.9 4.8 %multiply_reduce_fusion = (f32[512]{0:T(512)S(1)}, f32[1536]{0:T(1024)S(1)}, f32[1536]{0:T(1024)S(1)}, f32[1536,512]{1,0:T(8,128)S(1)}) fusion(bf16[8,4,48,512]{3,2,1,0:T(8,128)(2,1)} %all-to-all-done, f32[1536]{0:T(1024)S(1)} %rsqrt.15, f32[1536]{0:T(1024)S(1)} %div.33, f32[512]{0:T(512)S(1)} %copy-done.41, bf16[512,1024]{1,0:T(8,128)(2,1)} %param.17, ...), kind=kOutput, calls=%fused_computation.166 | convolution fusion | flops 1623978496 | bytes 8941568 | tf_op jit(solution)/shard_map/rf,df->rd/dot_general | solution.py:147
  275.8 3.4 select_convert_fusion
  279.2 5.2 %all-to-all-start.1 = ((bf16[8,4,48,512]{3,2,1,0:T(8,128)(2,1)}), bf16[8,4,48,512]{3,2,1,0:T(8,128)(2,1)}, u32[]{:S(2)}, u32[]{:S(2)}) async-start(bf16[8,4,48,512]{3,2,1,0:T(8,128)(2,1)} %bitcast.73), calls=%async_computation.1 | async-start | bytes 3145728 | tf_op jit(solution)/shard_map/all_to_all | solution.py:152
  284.4 0.6 dynamic-slice
  285.7 0.7 fusion.117
  286.5 4.5 fusion.102
  291.1 0.7 fusion.116
  291.8 0.2 compare_reduce_fusion.24
  292.0 16.2 %compare_and_fusion.1 = (pred[768]{0:T(1024)(128)(4,1)S(1)}, s32[768]{0:T(1024)S(1)}) fusion(s32[768]{0:T(1024)S(1)} %convert_reduce_fusion.1, pred[768]{0:T(1024)(128)(4,1)S(1)} %get-tuple-element.70, pred[768]{0:T(1024)(128)(4,1)S(1)} %get-tuple-element.68, pred[768]{0:T(1024)(128)(4,1)S(1)} %get-tuple-element.69, ...), kind=kLoop, calls=%fused_computation.315 | loop fusion | flops 32256 | bytes 29284 | tf_op jit(solution)/shard_map/jit(_take)/and | solution.py:125
  308.3 2.5 convolution_convert_fusion
  310.8 3.3 gather_fusion
  314.1 21.9 %all-reduce.2 = bf16[512]{0:T(512)(128)(2,1)S(1)} all-reduce(f32[512]{0:T(512)S(1)} %get-tuple-element.9), channel_id=5, replica_groups=mesh['dp'=4,'bucket'=8] {'bucket'}, use_global_device_ids=true, to_apply=%region_56.58.clone | all-reduce | flops 512 | bytes 3072
  336.1 2.2 broadcast_select_fusion.2
  338.3 0.8 copy.42
  339.1 5.9 %all-reduce.5 = (bf16[64,31]{0,1:T(8,128)(2,1)S(1)}, bf16[64]{0:T(256)(128)(2,1)S(1)}) all-reduce(bf16[64,31]{0,1:T(8,128)(2,1)S(1)} %copy.42, bf16[64]{0:T(256)(128)(2,1)S(1)} %dynamic-slice.3), channel_id=1, replica_groups=mesh['dp'=4,'bucket'=8] {'dp'}, use_global_device_ids=true, to_apply=%region_54.56 | all-reduce | flops 2048 | bytes 8192 | tf_op jit(solution)/shard_map/psum | solution.py:171
  345.0 0.5 convert_element_type.239
  345.6 0.6 convert_element_type.237
  346.2 7.7 %reduce-scatter.8.cloned.1.call-done = f32[64,512]{1,0:T(8,128)} async-done(((f32[512,512]{1,0:T(8,128)}), f32[64,512]{1,0:T(8,128)}) %reduce-scatter.8.cloned.1.call-update) | async-done | bytes 131088 | tf_op jit(solution)/shard_map/reduce_scatter | solution.py:164
  353.8 1.5 convert_element_type.233
  355.4 2.1 gather_fusion.3
  357.5 67.6 %reduce-scatter.6.cloned.1.call-done = f32[64,1024]{1,0:T(8,128)} async-done(((f32[512,1024]{1,0:T(8,128)}), f32[64,1024]{1,0:T(8,128)}) %reduce-scatter.6.cloned.1.call-update) | async-done | bytes 262160 | tf_op jit(solution)/shard_map/reduce_scatter | solution.py:163
  425.0 1.6 convert_element_type.231
  426.7 1.4 broadcast_select_fusion
  428.0 31.1 %all-reduce.9.cloned.1.call-done = (bf16[64,1024]{1,0:T(8,128)(2,1)}, bf16[64,512]{1,0:T(8,128)(2,1)}) async-done(((bf16[64,1024]{1,0:T(8,128)(2,1)}, bf16[64,512]{1,0:T(8,128)(2,1)}), (bf16[64,1024]{1,0:T(8,128)(2,1)}, bf16[64,512]{1,0:T(8,128)(2,1)})) %all-reduce.9.cloned.1.call-update) | async-done | bytes 196624 | tf_op jit(solution)/shard_map/psum | solution.py:169
  459.1 1.6 convert_element_type.232
  460.7 1.5 convert_element_type.234
  (146 shorter events, 1.9 us)
Async XLA Ops:
  7.2 3.6 copy-start
  12.6 10.2 %copy-start.46 = (s32[1,256]{1,0:T(1,128)S(1)}, s32[1,256]{1,0:T(1,128)}, u32[]{:S(2)}) copy-start(s32[1,256]{1,0:T(1,128)} %param.13) | copy-start | bytes 3076
  12.6 12.0 %copy-start.1 = (bf16[768,512]{1,0:T(8,128)(2,1)S(1)}, bf16[768,512]{1,0:T(8,128)(2,1)}, u32[]{:S(2)}) copy-start(bf16[768,512]{1,0:T(8,128)(2,1)} %param.15) | copy-start | bytes 2359300
  15.4 44.4 %all-to-all-start = ((bf16[8,4,48,512]{3,2,1,0:T(8,128)(2,1)}), bf16[8,4,48,512]{3,2,1,0:T(8,128)(2,1)}, u32[]{:S(2)}, u32[]{:S(2)}) async-start(bf16[8,4,48,512]{3,2,1,0:T(8,128)(2,1)} %bitcast.243), calls=%async_computation | async-start | bytes 3145728 | tf_op jit(solution)/shard_map/all_to_all | solution.py:84
  22.7 315.6 %reduce-scatter.10.cloned.1.call-start = ((), (), s32[]{:S(2)}) async-start(), calls=%async_computation.7 | async-start | bytes 294912
  24.5 5.4 %copy-start.9 = (f32[512,31]{0,1:T(8,128)S(1)}, f32[512,31]{0,1:T(8,128)}, u32[]{:S(2)}) copy-start(f32[512,31]{0,1:T(8,128)} %param.18) | copy-start | bytes 190468
  29.9 33.8 %copy-start.41 = (f32[512]{0:T(512)S(1)}, f32[512]{0:T(512)}, u32[]{:S(2)}) copy-start(f32[512]{0:T(512)} %param.16) | copy-start | bytes 6148
  30.0 103.4 %copy-start.45 = (pred[1536]{0:T(1024)(128)(4,1)}, pred[1536]{0:T(1024)(128)(4,1)S(1)}, u32[]{:S(2)}) copy-start(pred[1536]{0:T(1024)(128)(4,1)S(1)} %compare_and_fusion) | copy-start | bytes 4612
  30.1 35.7 %copy-start.47 = (bf16[512,1024]{1,0:T(8,128)(2,1)S(1)}, bf16[512,1024]{1,0:T(8,128)(2,1)}, u32[]{:S(2)}) copy-start(bf16[512,1024]{1,0:T(8,128)(2,1)} %param.17) | copy-start | bytes 3145732
  65.8 1.8 copy-start.6
  67.6 2.7 copy-start.3
  67.6 2.7 copy-start.10
  67.6 2.6 copy-start.11
  67.6 2.6 copy-start.12
  67.7 2.6 copy-start.13
  67.7 2.6 copy-start.14
  67.7 2.6 copy-start.15
  67.7 2.6 copy-start.16
  67.7 2.6 copy-start.17
  67.7 2.6 copy-start.18
  67.7 2.6 copy-start.19
  67.7 2.6 copy-start.20
  67.8 2.6 copy-start.21
  67.8 2.6 copy-start.22
  67.8 2.6 copy-start.23
  67.8 2.6 copy-start.24
  67.8 2.6 copy-start.25
  67.8 2.6 copy-start.26
  67.8 2.6 copy-start.27
  67.8 2.6 copy-start.28
  67.9 2.6 copy-start.29
  67.9 2.6 copy-start.30
  67.9 2.6 copy-start.31
  67.9 2.6 copy-start.32
  67.9 2.6 copy-start.33
  67.9 2.6 copy-start.34
  67.9 2.6 copy-start.35
  68.0 2.6 copy-start.36
  68.0 2.6 copy-start.37
  68.0 2.6 copy-start.38
  68.0 2.6 copy-start.39
  70.3 58.9 %copy-start.40 = (f32[512]{0:T(512)S(1)}, f32[512]{0:T(512)}, u32[]{:S(2)}) copy-start(f32[512]{0:T(512)} %param.19) | copy-start | bytes 6148
  70.3 58.9 %copy-start.42 = (f32[512]{0:T(512)S(1)}, f32[512]{0:T(512)}, u32[]{:S(2)}) copy-start(f32[512]{0:T(512)} %param.20) | copy-start | bytes 6148
  129.2 4.2 copy-start.5
  129.2 4.2 copy-start.48
  133.4 4.3 copy-start.4
  179.0 0.6 copy-start.43
  179.0 6.1 %copy-start.44 = (f32[512]{0:T(512)}, f32[512]{0:T(512)S(1)}, u32[]{:S(2)}) copy-start(f32[512]{0:T(512)S(1)} %get-tuple-element.72) | copy-start | bytes 6148
  185.2 15.7 %copy-start.2 = (f32[1536,512]{1,0:T(8,128)}, f32[1536,512]{1,0:T(8,128)S(1)}, u32[]{:S(2)}) copy-start(f32[1536,512]{1,0:T(8,128)S(1)} %get-tuple-element.80) | copy-start | bytes 9437188
  208.4 145.4 %reduce-scatter.8.cloned.1.call-start = ((), (), s32[]{:S(2)}) async-start(), calls=%async_computation.6 | async-start | bytes 1179648 | tf_op jit(solution)/shard_map/reduce_scatter | solution.py:164
  212.5 212.5 %reduce-scatter.6.cloned.1.call-start = ((), (), s32[]{:S(2)}) async-start(), calls=%async_computation.5 | async-start | bytes 2359296 | tf_op jit(solution)/shard_map/reduce_scatter | solution.py:163
  261.9 5.9 %copy-start.7 = (bf16[1536,512]{1,0:T(8,128)(2,1)S(1)}, bf16[1536,512]{1,0:T(8,128)(2,1)}, u32[]{:S(2)}) copy-start(bf16[1536,512]{1,0:T(8,128)(2,1)} %copy-done.6) | copy-start | bytes 4718596
  266.6 1.2 copy-start.8
  279.2 5.2 %copy-start.49 = (u32[32]{0:T(128)S(1)}, u32[32]{0:T(128)}, u32[]{:S(2)}) copy-start(u32[32]{0:T(128)} %constant.240) | copy-start | bytes 388
  279.2 76.2 %all-to-all-start.1 = ((bf16[8,4,48,512]{3,2,1,0:T(8,128)(2,1)}), bf16[8,4,48,512]{3,2,1,0:T(8,128)(2,1)}, u32[]{:S(2)}, u32[]{:S(2)}) async-start(bf16[8,4,48,512]{3,2,1,0:T(8,128)(2,1)} %bitcast.73), calls=%async_computation.1 | async-start | bytes 3145728 | tf_op jit(solution)/shard_map/all_to_all | solution.py:152
  284.4 174.7 %all-reduce.9.cloned.1.call-start = ((), (), s32[]{:S(2)}) async-start(), calls=%async_computation.8 | async-start | bytes 393216 | tf_op jit(solution)/shard_map/psum | solution.py:169
Sparse Core Ops, SparseCore 0:
  208.5 61.9 reduce-scatter.9
  273.9 79.8 reduce-scatter.7
  357.4 67.6 reduce-scatter.5
  427.9 31.1 all-reduce.8
where the time goes:
time: 470 us; the launch traced here: 469 us
  other arithmetic  155 us (33%)
  waiting for transfers between devices  136 us (29%)
  blocking collectives  107 us (23%)
  local copies, waits for them, and re-layouts  21.6 us (5%)
  matrix products  20.6 us (4%)
  between operations  15.4 us (3%)
  starting transfers between devices  12.8 us (3%)
    reduce_scatter x1, waiting for transfers between devices, local(): lax.psum_scatter(grad_win, 'bucket', scatter_dimension=0, tiled=True)  67.6 us
    add x1, other arithmetic, conv_backward(): grad_gated + jnp.where(same_back, grad_pad[:, back_start:back_start + len...  49.1 us
    psum x1, blocking collectives, local(): lax.psum((jnp.sum(grad_bn_rows, axis=0), jnp.sum(grad_bn_rows * bn_normed...  41.4 us
    psum x1, blocking collectives, local(): lax.psum((jnp.sum(masked, axis=0), jnp.sum(masked * masked, axis=0)), ('d...  37.9 us
    psum x1, waiting for transfers between devices, local(): lax.psum(row_sums[0].astype(jnp.bfloat16), 'dp').astype(jnp.float32)  31.1 us
    all_to_all x1, waiting for transfers between devices, local(): lax.all_to_all(outgoing, 'bucket', split_axis=0, concat_axis=0, tiled=True)  29.7 us
    reduce_sum x5, other arithmetic, conv_backward(): grad_cols.append(jnp.sum(shifted * grad_conv, axis=(0, 1)))  27.7 us
    unnamed x1, blocking collectives  21.9 us
  transfers between devices with their start and end apart: 6, of which 4 were waited for; matrix products, arithmetic and copies ran while one was open for 24% of the time, Pallas kernels for 0%

commit v1 on v0

--- a/solution.py
+++ b/solution.py
@@ -127,7 +127,10 @@
     grad_swish = jnp.einsum("re,de->rd", work_grad, w_out, preferred_element_type=jnp.float32)
     grad_bn_rows = grad_swish * (bn_sig * (1.0 + bn_value * (1.0 - bn_sig)))
     bias_total, gain_total = lax.psum(
-        (jnp.sum(grad_bn_rows, axis=0), jnp.sum(grad_bn_rows * bn_normed, axis=0)), ("dp", "bucket")
+        lax.psum(
+            (jnp.sum(grad_bn_rows, axis=0), jnp.sum(grad_bn_rows * bn_normed, axis=0)), "bucket"
+        ),
+        "dp",
     )
     grad_conv = jnp.where(
         slot_valid_flat[:, None],

time: 470 us -> 451 us (0.960)
  blocking collectives: 107 us -> 92.7 us
    psum x1, blocking collectives: 41.4 us -> 21.1 us  [local(): lax.psum((jnp.sum(grad_bn_rows, axis=0), jnp.sum(grad_bn_rows * bn_normed...]
    psum x0 -> x1, blocking collectives: none -> 5.95 us  [local(): lax.psum(lax.psum((jnp.sum(grad_bn_rows, axis=0), jnp.sum(grad_bn_rows *...]
  transfers between devices with their start and end apart: 6 -> 6, of which waited for: 4 -> 4; matrix products, arithmetic and copies ran while one was open for 24% -> 25% of each run, Pallas kernels for 0% -> 0%
where the time goes in v1:
time: 451 us; the launch traced here: 450 us
  other arithmetic  155 us (34%)
  waiting for transfers between devices  132 us (29%)
  blocking collectives  92.7 us (21%)
  local copies, waits for them, and re-layouts  21.6 us (5%)
  matrix products  20.6 us (5%)
  between operations  15.4 us (3%)
  starting transfers between devices  12.1 us (3%)
    reduce_scatter x1, waiting for transfers between devices, local(): lax.psum_scatter(grad_win, 'bucket', scatter_dimension=0, tiled=True)  67.5 us
    add x1, other arithmetic, conv_backward(): grad_gated + jnp.where(same_back, grad_pad[:, back_start:back_start + len...  49.1 us
    psum x1, blocking collectives, local(): lax.psum((jnp.sum(masked, axis=0), jnp.sum(masked * masked, axis=0)), ('d...  37.9 us
    psum x1, waiting for transfers between devices, local(): lax.psum(row_sums[0].astype(jnp.bfloat16), 'dp').astype(jnp.float32)  31 us
    all_to_all x1, waiting for transfers between devices, local(): lax.all_to_all(outgoing, 'bucket', split_axis=0, concat_axis=0, tiled=True)  29.7 us
    reduce_sum x5, other arithmetic, conv_backward(): grad_cols.append(jnp.sum(shifted * grad_conv, axis=(0, 1)))  27.7 us
    unnamed x1, blocking collectives  21.7 us
    psum x1, blocking collectives, local(): lax.psum((jnp.sum(grad_bn_rows, axis=0), jnp.sum(grad_bn_rows * bn_normed...  21.1 us
  transfers between devices with their start and end apart: 6, of which 4 were waited for; matrix products, arithmetic and copies ran while one was open for 25% of the time, Pallas kernels for 0%

profile of v1, /device:TPU:0, one launch (start us, length us, event | category | flops | bytes accessed | tf_op | source)
XLA Modules:
  0.0 449.9 jit_solution(7246657418253812164)
XLA Ops:
  7.2 0.5 broadcast.618
  7.7 1.3 reduce.68
  9.2 0.7 fusion.118
  10.0 0.7 scatter_custom_fusion
  10.8 1.8 gather_fusion.2
  12.6 2.8 broadcast_select_fusion.1
  15.4 7.3 %all-to-all-start = ((bf16[8,4,48,512]{3,2,1,0:T(8,128)(2,1)}), bf16[8,4,48,512]{3,2,1,0:T(8,128)(2,1)}, u32[]{:S(2)}, u32[]{:S(2)}) async-start(bf16[8,4,48,512]{3,2,1,0:T(8,128)(2,1)} %bitcast.243), calls=%async_computation | async-start | bytes 3145728 | tf_op jit(solution)/shard_map/all_to_all | solution.py:84
  22.7 0.7 reduce.69
  23.5 0.1 select_reduce_fusion.1
  24.1 0.1 reduce.7
  24.5 5.4 %gather_fusion.1 = bf16[1536,512]{1,0:T(8,128)(2,1)} fusion(bf16[768,512]{1,0:T(8,128)(2,1)S(1)} %copy-done.1, s32[2048]{0:T(1024)S(1)} %pad_clamp_fusion), kind=kCustom, calls=%fused_computation.3 | custom fusion | bytes 3151872 | tf_op jit(solution)/shard_map/jit(_take)/gather | solution.py:103
  30.1 29.7 %all-to-all-done = bf16[8,4,48,512]{3,2,1,0:T(8,128)(2,1)} async-done(((bf16[8,4,48,512]{3,2,1,0:T(8,128)(2,1)}), bf16[8,4,48,512]{3,2,1,0:T(8,128)(2,1)}, u32[]{:S(2)}, u32[]{:S(2)}) %all-to-all-start) | async-done | bytes 1572896 | tf_op jit(solution)/shard_map/all_to_all | solution.py:84
  59.8 1.7 convert_reduce_fusion
  61.6 2.1 multiply_reduce_fusion.35
  63.8 2.0 multiply_convert_fusion.3
  65.8 1.8 fusion.119
  68.0 1.4 select_convert_fusion.1
  69.4 0.9 copy-done.3
  70.6 20.7 %select_reduce_fusion = (f32[512]{0:T(512)S(1)}, f32[512]{0:T(512)S(1)}, f32[32,48,512]{2,1,0:T(8,128)}) fusion(pred[32,48]{1,0:T(8,128)(4,1)S(1)} %iota_compare_fusion.3, f32[512]{0:T(512)S(1)} %bitcast.355, pred[32,48]{1,0:T(8,128)(4,1)S(1)} %bitcast.323, f32[512]{0:T(512)S(1)} %bitcast.357, pred[32,48]{1,0:T(8,128)(4,1)S(1)} %bitcast.320, ...), kind=kLoop, calls=%fused_computation.243 | loop fusion | flops 99089408 | bytes 4833792 | tf_op jit(solution)/shard_map/reduce_sum | solution.py:115
  91.3 37.9 %all-reduce.3 = (f32[512]{0:T(512)S(1)}, f32[512]{0:T(512)S(1)}) all-reduce(f32[512]{0:T(512)S(1)} %get-tuple-element.42, f32[512]{0:T(512)S(1)} %get-tuple-element.41), channel_id=1, replica_groups=mesh['dp'=4,'bucket'=8] {'dp','bucket'}, use_global_device_ids=true, to_apply=%region_11.13 | all-reduce | flops 1024 | bytes 8192 | tf_op jit(solution)/shard_map/psum | solution.py:114
  129.2 4.2 multiply_convert_fusion.2
  133.4 4.3 fusion.111
  137.6 21.1 %all-reduce.4 = (f32[512]{0:T(512)S(1)}, f32[512]{0:T(512)S(1)}) all-reduce(f32[512]{0:T(512)S(1)} %get-tuple-element.45, f32[512]{0:T(512)S(1)} %get-tuple-element.44), channel_id=1, replica_groups=mesh['dp'=4,'bucket'=8] {'bucket'}, use_global_device_ids=true, to_apply=%region_16.18 | all-reduce | flops 1024 | bytes 8192 | tf_op jit(solution)/shard_map/psum | solution.py:130
  158.7 5.9 %all-reduce.5 = (f32[512]{0:T(512)S(1)}, f32[512]{0:T(512)S(1)}) all-reduce(f32[512]{0:T(512)S(1)} %get-tuple-element.73, f32[512]{0:T(512)S(1)} %get-tuple-element.74), channel_id=1, replica_groups=mesh['dp'=4,'bucket'=8] {'dp'}, use_global_device_ids=true, to_apply=%region_17.19 | all-reduce | flops 1024 | bytes 8192 | tf_op jit(solution)/shard_map/psum | solution.py:129
  164.7 0.6 copy-done.43
  165.3 5.5 %multiply_reduce_fusion.16 = (f32[512]{0:T(512)S(1)}, f32[1536,512]{1,0:T(8,128)S(1)}) fusion(f32[1536,512]{1,0:T(8,128)} %copy-done.4, f32[512]{0:T(512)S(1)} %get-tuple-element.166, f32[1536,512]{1,0:T(8,128)} %get-tuple-element.164, f32[512]{0:T(512)S(1)} %get-tuple-element.167, f32[512]{0:T(512)S(1)} %get-tuple-element.85, pred[1536]{0:T(1024)(128)(4,1)S(1)} %lt.126, ...), kind=kLoop, calls=%fused_computation.182 | loop fusion | flops 11009536 | bytes 15738368 | tf_op jit(solution)/shard_map/reduce_sum | solution.py:49
  170.8 1.9 multiply_reduce_fusion.29
  172.7 7.1 %multiply_reduce_fusion.10 = (f32[512]{0:T(512)S(1)}, f32[512]{0:T(512)S(1)}, f32[512]{0:T(512)S(1)}, f32[512]{0:T(512)S(1)}, f32[512]{0:T(512)S(1)}, /*index=5*...) fusion(f32[32,48,512]{2,1,0:T(8,128)S(1)} %bitcast.234, pred[32,48]{1,0:T(8,128)(4,1)S(1)} %bitcast.297, ...), kind=kLoop, calls=%fused_computation.176 | loop fusion | flops 28306944 | bytes 4750848 | tf_op jit(solution)/shard_map/reduce_sum | solution.py:49
  179.9 6.7 %multiply_reduce_fusion.20 = (f32[512]{0:T(512)S(1)}, f32[512]{0:T(512)S(1)}, f32[512]{0:T(512)S(1)}, f32[512]{0:T(512)S(1)}, f32[512]{0:T(512)S(1)}, /*index=5*...) fusion(f32[32,48,512]{2,1,0:T(8,128)S(1)} %bitcast.235, pred[32,48]{1,0:T(8,128)(4,1)S(1)} %bitcast.270, ...), kind=kLoop, calls=%fused_computation.186 | loop fusion | flops 28306944 | bytes 4750848 | tf_op jit(solution)/shard_map/reduce_sum | solution.py:49
  186.6 6.5 %multiply_reduce_fusion.1 = (f32[512]{0:T(512)S(1)}, f32[512]{0:T(512)S(1)}, f32[512]{0:T(512)S(1)}, f32[512]{0:T(512)S(1)}, f32[512]{0:T(512)S(1)}, /*index=5*/...) fusion(f32[32,48,512]{2,1,0:T(8,128)S(1)} %bitcast.236, pred[32,48]{1,0:T(8,128)(4,1)S(1)} %bitcast.324, ...), kind=kLoop, calls=%fused_computation.167 | loop fusion | flops 28306944 | bytes 4750848 | tf_op jit(solution)/shard_map/reduce_sum | solution.py:49
  193.1 0.1 stack.127
  193.2 0.8 copy.41
  194.1 4.0 fusion.110
  198.2 0.3 reduce-scatter.6.cloned.1.call-start
  198.5 49.1 %fusion.73 = f32[32,48,512]{2,1,0:T(8,128)} fusion(f32[32,48,512]{2,1,0:T(8,128)} %bitcast.237, f32[512]{0:T(512)S(1)} %bitcast.356, f32[512]{0:T(512)S(1)} %bitcast.358, f32[512]{0:T(512)S(1)} %bitcast.362, f32[512]{0:T(512)S(1)} %bitcast.364, f32[512]{0:T(512)S(1)} %bitcast.366, f32[512]{0:T(512)S(1)} %bitcast.368, f32[512]{0:T(512)S(1)} %bitcast.370, ...), kind=kLoop, calls=%fused_computation.139 | loop fusion | flops 71565312 | bytes 6401024 | tf_op jit(solution)/shard_map/add | solution.py:53
  247.5 4.7 %multiply_convert_fusion.1 = (bf16[1536,512]{1,0:T(8,128)(2,1)S(1)}, bf16[1536,512]{1,0:T(8,128)(2,1)S(1)}) fusion(f32[32,48,512]{2,1,0:T(8,128)} %fusion.73, pred[1536]{0:T(1024)(128)(4,1)S(1)} %lt.126, f32[1536,1024]{1,0:T(8,128)} %copy-done.3), kind=kLoop, calls=%fused_computation.201 | loop fusion | flops 8650752 | bytes 12584448 | tf_op jit(solution)/shard_map/convert.1
  252.2 1.1 copy-done.8
  253.4 3.2 fusion.95
  256.6 4.8 %multiply_reduce_fusion = (f32[512]{0:T(512)S(1)}, f32[1536]{0:T(1024)S(1)}, f32[1536]{0:T(1024)S(1)}, f32[1536,512]{1,0:T(8,128)S(1)}) fusion(bf16[8,4,48,512]{3,2,1,0:T(8,128)(2,1)} %all-to-all-done, f32[1536]{0:T(1024)S(1)} %rsqrt.15, f32[1536]{0:T(1024)S(1)} %div.33, f32[512]{0:T(512)S(1)} %copy-done.41, bf16[512,1024]{1,0:T(8,128)(2,1)} %param.17, ...), kind=kOutput, calls=%fused_computation.166 | convolution fusion | flops 1623978496 | bytes 8941568 | tf_op jit(solution)/shard_map/rf,df->rd/dot_general | solution.py:150
  261.4 3.5 select_convert_fusion
  264.9 4.4 all-to-all-start.1
  269.4 0.6 dynamic-slice
  270.7 0.7 fusion.117
  271.5 4.5 %fusion.102 = (s32[768]{0:T(1024)S(1)}, s32[768,1]{0,1:T(1,128)S(1)}) fusion(s32[]{:T(128)} %bitcast.25, s32[]{:T(128)} %bitcast.26, s32[]{:T(128)} %bitcast.27, s32[]{:T(128)} %bitcast.28, s32[]{:T(128)} %bitcast.29, s32[]{:T(128)} %bitcast.31, s32[]{:T(128)} %bitcast.30, s32[768]{0:T(1024)S(1)} %get-tuple-element.128, s32[768]{0:T(1024)S(1)} %get-tuple-element.127), kind=kLoop, calls=%fused_computation.316 | loop fusion | flops 10752 | bytes 12316 | tf_op jit(solution)/shard_map/jit(_take)/gather | solution.py:94
  276.0 0.7 fusion.116
  276.8 0.2 compare_reduce_fusion.24
  277.0 16.2 %compare_and_fusion.1 = (pred[768]{0:T(1024)(128)(4,1)S(1)}, s32[768]{0:T(1024)S(1)}) fusion(s32[768]{0:T(1024)S(1)} %convert_reduce_fusion.1, pred[768]{0:T(1024)(128)(4,1)S(1)} %get-tuple-element.70, pred[768]{0:T(1024)(128)(4,1)S(1)} %get-tuple-element.68, pred[768]{0:T(1024)(128)(4,1)S(1)} %get-tuple-element.69, ...), kind=kLoop, calls=%fused_computation.315 | loop fusion | flops 32256 | bytes 29284 | tf_op jit(solution)/shard_map/jit(_take)/and | solution.py:125
  293.3 2.5 convolution_convert_fusion
  295.7 3.3 gather_fusion
  299.1 21.7 %all-reduce.2 = bf16[512]{0:T(512)(128)(2,1)S(1)} all-reduce(f32[512]{0:T(512)S(1)} %get-tuple-element.9), channel_id=5, replica_groups=mesh['dp'=4,'bucket'=8] {'bucket'}, use_global_device_ids=true, to_apply=%region_58.60.clone | all-reduce | flops 512 | bytes 3072
  320.9 2.2 broadcast_select_fusion.2
  323.1 0.8 copy.42
  323.9 6.1 %all-reduce.6 = (bf16[64,31]{0,1:T(8,128)(2,1)S(1)}, bf16[64]{0:T(256)(128)(2,1)S(1)}) all-reduce(bf16[64,31]{0,1:T(8,128)(2,1)S(1)} %copy.42, bf16[64]{0:T(256)(128)(2,1)S(1)} %dynamic-slice.3), channel_id=1, replica_groups=mesh['dp'=4,'bucket'=8] {'dp'}, use_global_device_ids=true, to_apply=%region_56.58 | all-reduce | flops 2048 | bytes 8192 | tf_op jit(solution)/shard_map/psum | solution.py:174
  330.0 0.5 convert_element_type.239
  330.5 0.6 convert_element_type.237
  331.1 4.1 reduce-scatter.8.cloned.1.call-done
  335.2 1.5 convert_element_type.233
  336.8 2.1 gather_fusion.3
  338.8 67.5 %reduce-scatter.6.cloned.1.call-done = f32[64,1024]{1,0:T(8,128)} async-done(((f32[512,1024]{1,0:T(8,128)}), f32[64,1024]{1,0:T(8,128)}) %reduce-scatter.6.cloned.1.call-update) | async-done | bytes 262160 | tf_op jit(solution)/shard_map/reduce_scatter | solution.py:166
  406.3 1.6 convert_element_type.231
  407.9 1.4 broadcast_select_fusion
  409.3 31.0 %all-reduce.10.cloned.1.call-done = (bf16[64,1024]{1,0:T(8,128)(2,1)}, bf16[64,512]{1,0:T(8,128)(2,1)}) async-done(((bf16[64,1024]{1,0:T(8,128)(2,1)}, bf16[64,512]{1,0:T(8,128)(2,1)}), (bf16[64,1024]{1,0:T(8,128)(2,1)}, bf16[64,512]{1,0:T(8,128)(2,1)})) %all-reduce.10.cloned.1.call-update) | async-done | bytes 196624 | tf_op jit(solution)/shard_map/psum | solution.py:172
  440.2 1.6 convert_element_type.232
  441.9 1.5 convert_element_type.234
  (147 shorter events, 2.0 us)
Async XLA Ops:
  7.2 3.6 copy-start
  12.6 10.2 %copy-start.46 = (s32[1,256]{1,0:T(1,128)S(1)}, s32[1,256]{1,0:T(1,128)}, u32[]{:S(2)}) copy-start(s32[1,256]{1,0:T(1,128)} %param.13) | copy-start | bytes 3076
  12.6 12.0 %copy-start.1 = (bf16[768,512]{1,0:T(8,128)(2,1)S(1)}, bf16[768,512]{1,0:T(8,128)(2,1)}, u32[]{:S(2)}) copy-start(bf16[768,512]{1,0:T(8,128)(2,1)} %param.15) | copy-start | bytes 2359300
  15.4 44.4 %all-to-all-start = ((bf16[8,4,48,512]{3,2,1,0:T(8,128)(2,1)}), bf16[8,4,48,512]{3,2,1,0:T(8,128)(2,1)}, u32[]{:S(2)}, u32[]{:S(2)}) async-start(bf16[8,4,48,512]{3,2,1,0:T(8,128)(2,1)} %bitcast.243), calls=%async_computation | async-start | bytes 3145728 | tf_op jit(solution)/shard_map/all_to_all | solution.py:84
  22.7 300.4 %reduce-scatter.10.cloned.1.call-start = ((), (), s32[]{:S(2)}) async-start(), calls=%async_computation.7 | async-start | bytes 294912
  24.5 5.4 %copy-start.9 = (f32[512,31]{0,1:T(8,128)S(1)}, f32[512,31]{0,1:T(8,128)}, u32[]{:S(2)}) copy-start(f32[512,31]{0,1:T(8,128)} %param.18) | copy-start | bytes 190468
  29.9 33.8 %copy-start.41 = (f32[512]{0:T(512)S(1)}, f32[512]{0:T(512)}, u32[]{:S(2)}) copy-start(f32[512]{0:T(512)} %param.16) | copy-start | bytes 6148
  30.0 103.4 %copy-start.45 = (pred[1536]{0:T(1024)(128)(4,1)}, pred[1536]{0:T(1024)(128)(4,1)S(1)}, u32[]{:S(2)}) copy-start(pred[1536]{0:T(1024)(128)(4,1)S(1)} %compare_and_fusion) | copy-start | bytes 4612
  30.1 35.7 %copy-start.47 = (bf16[512,1024]{1,0:T(8,128)(2,1)S(1)}, bf16[512,1024]{1,0:T(8,128)(2,1)}, u32[]{:S(2)}) copy-start(bf16[512,1024]{1,0:T(8,128)(2,1)} %param.17) | copy-start | bytes 3145732
  65.8 1.8 copy-start.6
  67.6 2.7 copy-start.3
  67.6 2.7 copy-start.10
  67.6 2.6 copy-start.11
  67.6 2.6 copy-start.12
  67.7 2.6 copy-start.13
  67.7 2.6 copy-start.14
  67.7 2.6 copy-start.15
  67.7 2.6 copy-start.16
  67.7 2.6 copy-start.17
  67.7 2.6 copy-start.18
  67.7 2.6 copy-start.19
  67.7 2.6 copy-start.20
  67.8 2.6 copy-start.21
  67.8 2.6 copy-start.22
  67.8 2.6 copy-start.23
  67.8 2.6 copy-start.24
  67.8 2.6 copy-start.25
  67.8 2.6 copy-start.26
  67.8 2.6 copy-start.27
  67.8 2.6 copy-start.28
  67.9 2.6 copy-start.29
  67.9 2.6 copy-start.30
  67.9 2.6 copy-start.31
  67.9 2.6 copy-start.32
  67.9 2.6 copy-start.33
  67.9 2.6 copy-start.34
  67.9 2.6 copy-start.35
  68.0 2.6 copy-start.36
  68.0 2.6 copy-start.37
  68.0 2.6 copy-start.38
  68.0 2.6 copy-start.39
  70.3 58.9 %copy-start.40 = (f32[512]{0:T(512)S(1)}, f32[512]{0:T(512)}, u32[]{:S(2)}) copy-start(f32[512]{0:T(512)} %param.19) | copy-start | bytes 6148
  70.3 58.9 %copy-start.42 = (f32[512]{0:T(512)S(1)}, f32[512]{0:T(512)}, u32[]{:S(2)}) copy-start(f32[512]{0:T(512)} %param.20) | copy-start | bytes 6148
  129.2 4.2 copy-start.5
  129.2 4.2 copy-start.48
  133.3 4.3 copy-start.4
  164.7 0.6 copy-start.43
  164.7 6.1 %copy-start.44 = (f32[512]{0:T(512)}, f32[512]{0:T(512)S(1)}, u32[]{:S(2)}) copy-start(f32[512]{0:T(512)S(1)} %get-tuple-element.76) | copy-start | bytes 6148
  170.8 15.7 %copy-start.2 = (f32[1536,512]{1,0:T(8,128)}, f32[1536,512]{1,0:T(8,128)S(1)}, u32[]{:S(2)}) copy-start(f32[1536,512]{1,0:T(8,128)S(1)} %get-tuple-element.82) | copy-start | bytes 9437188
  194.1 141.1 %reduce-scatter.8.cloned.1.call-start = ((), (), s32[]{:S(2)}) async-start(), calls=%async_computation.6 | async-start | bytes 1179648 | tf_op jit(solution)/shard_map/reduce_scatter | solution.py:167
  198.2 208.1 %reduce-scatter.6.cloned.1.call-start = ((), (), s32[]{:S(2)}) async-start(), calls=%async_computation.5 | async-start | bytes 2359296 | tf_op jit(solution)/shard_map/reduce_scatter | solution.py:166
  247.5 5.9 %copy-start.7 = (bf16[1536,512]{1,0:T(8,128)(2,1)S(1)}, bf16[1536,512]{1,0:T(8,128)(2,1)}, u32[]{:S(2)}) copy-start(bf16[1536,512]{1,0:T(8,128)(2,1)} %copy-done.6) | copy-start | bytes 4718596
  252.2 1.2 copy-start.8
  264.9 4.5 %copy-start.49 = (u32[32]{0:T(128)S(1)}, u32[32]{0:T(128)}, u32[]{:S(2)}) copy-start(u32[32]{0:T(128)} %constant.240) | copy-start | bytes 388
  264.9 71.9 %all-to-all-start.1 = ((bf16[8,4,48,512]{3,2,1,0:T(8,128)(2,1)}), bf16[8,4,48,512]{3,2,1,0:T(8,128)(2,1)}, u32[]{:S(2)}, u32[]{:S(2)}) async-start(bf16[8,4,48,512]{3,2,1,0:T(8,128)(2,1)} %bitcast.73), calls=%async_computation.1 | async-start | bytes 3145728 | tf_op jit(solution)/shard_map/all_to_all | solution.py:155
  269.3 170.9 %all-reduce.10.cloned.1.call-start = ((), (), s32[]{:S(2)}) async-start(), calls=%async_computation.8 | async-start | bytes 393216 | tf_op jit(solution)/shard_map/psum | solution.py:172
Sparse Core Ops, SparseCore 0:
  194.2 58.1 reduce-scatter.9
  255.8 79.3 reduce-scatter.7
  338.7 67.4 reduce-scatter.5
  409.1 31.0 all-reduce.9
